TPU v7x, 512 devices: a whole 4x8x8 slice. The times are simulated.
512 devices in a mesh: leaf: 8 (over z), row: 8 (over y), col: 8 (over x, core).
Axes of the slice: x: 4, y: 8, z: 8, core: 2. Of those that a mesh axis runs over, the one named last changes fastest.
Arguments:
- child_inverse: bfloat16 [8, 2, 3072, 3072], P('leaf', None, 'row', 'col'), as said below
- child_rhs: bfloat16 [8, 2, 3072, 256], P('leaf', None, 'col'), may hold values from -6 to 6
- child_to_mid: bfloat16 [8, 2, 2048, 3072], P('leaf', None, ('row', 'col')), may hold values from -0.109375 to 0.109375
- child_to_root: bfloat16 [8, 2, 2048, 3072], P('leaf', None, ('row', 'col')), may hold values from -0.109375 to 0.109375
- mid_rows_list: int32 [8, 2, 2048], P('leaf'), may hold values from 0 to 4095, as said below
- root_rows_list: int32 [8, 2, 2048], P('leaf'), may hold values from 0 to 8191, as said below
- mid_inverse: bfloat16 [8, 4096, 4096], P('leaf', 'row', 'col'), as said below
- mid_rhs: bfloat16 [8, 4096, 256], P('leaf', 'col'), may hold values from -6 to 6
- mid_to_root: bfloat16 [8, 2048, 4096], P('leaf', ('row', 'col')), may hold values from -0.09375 to 0.09375
- mid_root_list: int32 [8, 2048], P('leaf'), may hold values from 0 to 8191, as said below
- root_inverse: bfloat16 [8192, 8192], P(('leaf', 'row'), 'col'), as said below
- root_rhs: bfloat16 [8192, 256], P('col'), may hold values from -6 to 6
Outputs:
- child_solution: bfloat16 [8, 2, 3072, 256], P('leaf', None, 'row')
- mid_solution: bfloat16 [8, 4096, 256], P('leaf', 'row')
- root_solution: bfloat16 [8192, 256], P(('leaf', 'row'))
Inputs may be any that keep to these rules, and one draw needn't show every extreme that they name: `mid_rows_list`: each list of a child holds 2048 distinct rows of its middle supernode in increasing order, always with the first and the last. `root_rows_list`: each list of a child holds 2048 distinct rows of the root in increasing order, always with the first and the last. `mid_root_list`: each list holds 2048 distinct rows of the root in increasing order, always with the first and the last. `child_inverse`: lower triangular with a positive diagonal. `mid_inverse`: lower triangular with a positive diagonal. `root_inverse`: lower triangular with a positive diagonal.
All inputs are finite; a program needn't handle non-finite values.
Results may differ from a plain program's by a relative error of at most 0.0085.
Values may be sent and summed in bfloat16 or wider, within the bound.
A program may use at most 64 MiB of HBM per device.

v0:
```python
import jax
import jax.numpy as jnp
from jax import lax
from jax.sharding import PartitionSpec as P


def solve_spread(partial_value):
    placed = lax.psum(partial_value, "col").astype(jnp.bfloat16)
    whole_rows = lax.all_gather(placed, "row", axis=2, tiled=True)
    return (placed, whole_rows)


def gather_updates(pieces):
    return lax.all_gather(pieces, ("row", "col"), axis=2, tiled=True)


def scatter_block(values, rows_list, piece_rows, col_index):
    width = values.shape[-1]
    flat_values = values.reshape(-1, width).astype(jnp.float32)
    offsets = rows_list.reshape(-1) - col_index * piece_rows
    inside = (offsets >= 0) & (offsets < piece_rows)
    target = jnp.where(inside, offsets, piece_rows)
    summed = jnp.zeros((piece_rows + 1, width), jnp.float32).at[target].add(flat_values)
    return summed[:piece_rows]


def per_device(
    child_inverse,
    child_rhs,
    child_to_mid,
    child_to_root,
    mid_rows_list,
    root_rows_list,
    mid_inverse,
    mid_rhs,
    mid_to_root,
    mid_root_list,
    root_inverse,
    root_rhs,
):
    grid_size = lax.axis_size("row") * lax.axis_size("col")
    col_index = lax.axis_index("col")
    rhs_width = child_rhs.shape[3]
    child_partial = jnp.einsum(
        "gcij,gcjr->gcir", child_inverse, child_rhs, preferred_element_type=jnp.float32
    )
    child_local, child_whole = solve_spread(child_partial)
    mid_piece = child_to_mid.shape[2]
    root_piece = child_to_root.shape[2]
    update_mid = jnp.einsum(
        "gcuj,gcjr->gcur", child_to_mid, child_whole, preferred_element_type=jnp.float32
    ).astype(jnp.bfloat16)
    update_root = jnp.einsum(
        "gcuj,gcjr->gcur", child_to_root, child_whole, preferred_element_type=jnp.float32
    ).astype(jnp.bfloat16)
    stacked = jnp.concatenate((update_mid, update_root), axis=2)
    gathered = gather_updates(stacked)
    lead_count = gathered.shape[0]
    child_count = gathered.shape[1]
    split_view = gathered.reshape(
        lead_count, child_count, grid_size, mid_piece + root_piece, rhs_width
    )
    mid_updates = split_view[:, :, :, :mid_piece].reshape(
        lead_count, child_count, grid_size * mid_piece, rhs_width
    )
    root_updates = split_view[:, :, :, mid_piece:].reshape(
        lead_count, child_count, grid_size * root_piece, rhs_width
    )
    root_group = root_rhs.shape[0]
    child_root_term = scatter_block(root_updates, root_rows_list, root_group, col_index)
    mid_term = scatter_block(mid_updates, mid_rows_list, mid_rhs.shape[1], col_index)
    mid_input = (mid_rhs[0].astype(jnp.float32) - mid_term).astype(jnp.bfloat16)
    mid_partial = jnp.dot(mid_inverse[0], mid_input, preferred_element_type=jnp.float32)[None, None]
    mid_local, mid_whole = solve_spread(mid_partial)
    update_top = jnp.dot(
        mid_to_root[0], mid_whole[0, 0], preferred_element_type=jnp.float32
    ).astype(jnp.bfloat16)[None, None]
    top_whole = gather_updates(update_top)
    top_term = scatter_block(top_whole, mid_root_list, root_group, col_index)
    root_sum = lax.psum(child_root_term + top_term, "leaf")
    root_input = (root_rhs.astype(jnp.float32) - root_sum).astype(jnp.bfloat16)
    root_partial = jnp.dot(root_inverse, root_input, preferred_element_type=jnp.float32)
    root_solution = lax.psum(root_partial, "col").astype(jnp.bfloat16)
    return (child_local, mid_local[0], root_solution)


def solution(mesh):
    in_specs = (
        P("leaf", None, "row", "col"),
        P("leaf", None, "col", None),
        P("leaf", None, ("row", "col"), None),
        P("leaf", None, ("row", "col"), None),
        P("leaf", None, None),
        P("leaf", None, None),
        P("leaf", "row", "col"),
        P("leaf", "col", None),
        P("leaf", ("row", "col"), None),
        P("leaf", None),
        P(("leaf", "row"), "col"),
        P("col", None),
    )
    out_specs = (P("leaf", None, "row", None), P("leaf", "row", None), P(("leaf", "row"), None))
    return jax.shard_map(
        per_device, mesh=mesh, in_specs=in_specs, out_specs=out_specs, check_vma=False
    )
```

profile of v0, /device:TPU:1, one launch (start us, length us, event | category | flops | bytes accessed | tf_op | source)
XLA Modules:
  0.0 499.2 jit_solution(5121878186767649496)
XLA Ops:
  7.2 1.0 copy-done
  8.2 1.4 convolution_bitcast_fusion
  9.6 33.4 %all-reduce.6 = bf16[1,2,384,256]{3,2,1,0:T(8,128)(2,1)} all-reduce(f32[1,2,384,256]{3,2,1,0:T(8,128)S(1)} %convolution_bitcast_fusion), channel_id=1, replica_groups=mesh['leaf'=8,'row'=8,'col'=8] {'col'}, use_global_device_ids=true, to_apply=%region_0.0 | all-reduce | flops 196608 | bytes 1179648 | tf_op jit(solution)/shard_map/psum | solution.py:8
  43.0 48.7 %all-gather.6.cloned.1.call-done = bf16[1,2,3072,256]{3,2,1,0:T(8,128)(2,1)} async-done(((bf16[1,2,384,256]{3,2,1,0:T(8,128)(2,1)}), bf16[1,2,3072,256]{3,2,1,0:T(8,128)(2,1)}) %all-gather.6.cloned.1.call-update) | async-done | bytes 3145744 | tf_op jit(solution)/shard_map/all_gather | solution.py:9
  91.8 2.7 fusion.18
  94.5 0.1 copy-done.1
  94.6 0.6 fusion.21
  95.2 0.6 pad_maximum_fusion
  96.1 84.4 %all-gather.8.cloned.1.call-done = bf16[1,2,4096,256]{3,2,1,0:T(8,128)(2,1)} async-done(((bf16[1,2,64,256]{3,2,1,0:T(8,128)(2,1)}), bf16[1,2,4096,256]{3,2,1,0:T(8,128)(2,1)}) %all-gather.8.cloned.1.call-update) | async-done | bytes 4194320 | tf_op jit(solution)/shard_map/all_gather | solution.py:14
  180.5 4.2 fusion.42
  184.7 28.3 %scatter_custom_fusion = f32[513,256]{1,0:T(8,128)S(1)} fusion(s32[4096]{0:T(1024)S(1)} %bitcast.88, bf16[4096,256]{1,0:T(8,128)(2,1)} %bitcast.83, f32[]{:T(128)} %constant.7.clone.1), kind=kCustom, calls=%fused_computation.5 | custom fusion | flops 2097152 | bytes 2622468 | tf_op jit(solution)/shard_map/scatter-add | solution.py:23
  213.0 2.2 convolution_bitcast_fusion.1
  215.2 27.8 %all-reduce.7 = bf16[1,1,512,256]{2,3,1,0:T(8,128)(2,1)} all-reduce(f32[1,1,512,256]{2,3,1,0:T(8,128)} %convolution_bitcast_fusion.1), channel_id=1, replica_groups=mesh['leaf'=8,'row'=8,'col'=8] {'col'}, use_global_device_ids=true, to_apply=%region_2.3 | all-reduce | flops 131072 | bytes 786432 | tf_op jit(solution)/shard_map/psum | solution.py:8
  243.1 39.4 %all-gather.10.cloned.1.call-done = bf16[1,1,4096,256]{2,3,1,0:T(8,128)(2,1)} async-done(((bf16[1,1,512,256]{2,3,1,0:T(8,128)(2,1)}), bf16[1,1,4096,256]{2,3,1,0:T(8,128)(2,1)}) %all-gather.10.cloned.1.call-update) | async-done | bytes 2097168 | tf_op jit(solution)/shard_map/all_gather | solution.py:9
  282.5 2.9 fusion.27
  285.7 29.1 %scatter_custom_fusion.1 = f32[1025,256]{1,0:T(8,128)} fusion(s32[4096]{0:T(1024)S(1)} %bitcast.89, bf16[4096,256]{1,0:T(8,128)(2,1)S(1)} %bitcast.82, f32[]{:T(128)} %constant.7.clone.1), kind=kCustom, calls=%fused_computation.3 | custom fusion | flops 2097152 | bytes 3146756 | tf_op jit(solution)/shard_map/scatter-add | solution.py:23
  314.8 56.8 %all-gather.12.cloned.1.call-done = bf16[2048,256]{1,0:T(8,128)(2,1)} async-done(((bf16[32,256]{1,0:T(8,128)(2,1)}), bf16[2048,256]{1,0:T(8,128)(2,1)}) %all-gather.12.cloned.1.call-update) | async-done | bytes 1048592 | tf_op jit(solution)/shard_map/all_gather | solution.py:14
  371.6 14.8 %scatter_custom_fusion.2 = f32[1025,256]{1,0:T(8,128)S(1)} fusion(s32[2048]{0:T(1024)S(1)} %bitcast.90, bf16[2048,256]{1,0:T(8,128)(2,1)} %all-gather.12.cloned.1.call-done, f32[]{:T(128)} %constant.7.clone.1), kind=kCustom, calls=%fused_computation.13 | custom fusion | flops 1048576 | bytes 2098180 | tf_op jit(solution)/shard_map/scatter-add | solution.py:23
  386.5 1.2 slice_add_fusion
  387.7 0.8 copy.17
  388.6 74.9 %all-reduce.5.cloned.1.call-done = f32[1024,256]{1,0:T(8,128)} async-done(((f32[1024,256]{1,0:T(8,128)}), f32[1024,256]{1,0:T(8,128)}) %all-reduce.5.cloned.1.call-update) | async-done | bytes 1048592 | tf_op jit(solution)/shard_map/psum | solution.py:80
  463.5 1.6 convolution_bitcast_fusion.2
  465.1 26.8 %all-reduce.8 = bf16[128,256]{0,1:T(8,128)(2,1)S(1)} all-reduce(f32[128,256]{0,1:T(8,128)S(1)} %convolution_bitcast_fusion.2), channel_id=1, replica_groups=mesh['leaf'=8,'row'=8,'col'=8] {'col'}, use_global_device_ids=true, to_apply=%region_6.7 | all-reduce | flops 32768 | bytes 196608 | tf_op jit(solution)/shard_map/psum | solution.py:83
  491.9 0.7 copy.18
  (37 shorter events, 0.5 us)
Async XLA Ops:
  7.2 1.1 copy-start
  7.2 84.6 %copy-start.5 = (bf16[1,2,32,3072]{3,2,1,0:T(8,128)(2,1)S(1)}, bf16[1,2,32,3072]{3,2,1,0:T(8,128)(2,1)}, u32[]{:S(2)}) copy-start(bf16[1,2,32,3072]{3,2,1,0:T(8,128)(2,1)} %param.14) | copy-start | bytes 1179652
  7.2 84.6 %all-gather.6.cloned.1.call-start = ((), (), s32[]{:S(2)}) async-start(), calls=%async_computation | async-start | bytes 3538944 | tf_op jit(solution)/shard_map/all_gather | solution.py:9
  43.0 51.5 %copy-start.6 = (bf16[1,2,32,3072]{3,2,1,0:T(8,128)(2,1)S(1)}, bf16[1,2,32,3072]{3,2,1,0:T(8,128)(2,1)}, u32[]{:S(2)}) copy-start(bf16[1,2,32,3072]{3,2,1,0:T(8,128)(2,1)} %param.15) | copy-start | bytes 1179652
  43.0 137.5 %all-gather.8.cloned.1.call-start = ((), (), s32[]{:S(2)}) async-start(), calls=%async_computation.1 | async-start | bytes 4259840 | tf_op jit(solution)/shard_map/all_gather | solution.py:14
  91.8 2.8 copy-start.1
  94.6 1.4 copy-start.8
  95.9 186.6 %all-gather.10.cloned.1.call-start = ((), (), s32[]{:S(2)}) async-start(), calls=%async_computation.2 | async-start | bytes 2359296 | tf_op jit(solution)/shard_map/all_gather | solution.py:9
  184.7 28.4 %copy-start.7 = (bf16[1,512,256]{2,1,0:T(8,128)(2,1)S(1)}, bf16[1,512,256]{2,1,0:T(8,128)(2,1)}, u32[]{:S(2)}) copy-start(bf16[1,512,256]{2,1,0:T(8,128)(2,1)} %param.19) | copy-start | bytes 786436
  215.2 70.3 %copy-start.9 = (s32[1,2,2048]{2,1,0:T(2,128)S(1)}, s32[1,2,2048]{2,1,0:T(2,128)}, u32[]{:S(2)}) copy-start(s32[1,2,2048]{2,1,0:T(2,128)} %param.17) | copy-start | bytes 49156
  215.2 70.4 %copy-start.10 = (s32[1,2048]{1,0:T(1,128)S(1)}, s32[1,2048]{1,0:T(1,128)}, u32[]{:S(2)}) copy-start(s32[1,2048]{1,0:T(1,128)} %param.21) | copy-start | bytes 24580
  243.1 128.6 %all-gather.12.cloned.1.call-start = ((), (), s32[]{:S(2)}) async-start(), calls=%async_computation.4 | async-start | bytes 1064960 | tf_op jit(solution)/shard_map/all_gather | solution.py:14
  285.5 178.0 %all-reduce.5.cloned.1.call-start = ((), (), s32[]{:S(2)}) async-start(), calls=%async_computation.3 | async-start | bytes 2097152 | tf_op jit(solution)/shard_map/psum | solution.py:80
  314.8 71.6 %copy-start.2 = (f32[1025,256]{1,0:T(8,128)S(1)}, f32[1025,256]{1,0:T(8,128)}, u32[]{:S(2)}) copy-start(f32[1025,256]{1,0:T(8,128)} %scatter_custom_fusion.1) | copy-start | bytes 3148804
  386.5 1.2 copy-start.3
  386.5 77.0 %copy-start.4 = (bf16[1024,256]{1,0:T(8,128)(2,1)S(1)}, bf16[1024,256]{1,0:T(8,128)(2,1)}, u32[]{:S(2)}) copy-start(bf16[1024,256]{1,0:T(8,128)(2,1)} %param.23) | copy-start | bytes 1572868
Sparse Core Ops, SparseCore 0:
  43.1 48.5 all-gather.5
  96.0 84.3 all-gather.7
  243.2 39.3 all-gather.9
  286.3 85.2 all-gather.11
  387.8 75.5 all-reduce.4
where the time goes:
time: 501 us; the launch traced here: 499 us
  waiting for transfers between devices  304 us (61%)
  blocking collectives  88 us (18%)
  other arithmetic  74.2 us (15%)
  between operations  14 us (3%)
  matrix products  11.4 us (2%)
  local copies, waits for them, and re-layouts  7.04 us (1%)
    all_gather x2, waiting for transfers between devices, gather_updates(): return lax.all_gather(pieces, ('row', 'col'), axis=2, tiled=True)  141 us
    all_gather x2, waiting for transfers between devices, solve_spread(): whole_rows = lax.all_gather(placed, 'row', axis=2, tiled=True)  88.1 us
    psum x1, waiting for transfers between devices, per_device(): root_sum = lax.psum(child_root_term + top_term, 'leaf')  74.9 us
    scatter-add x3, other arithmetic, scatter_block(): jnp.zeros((piece_rows + 1, width), jnp.float32).at[target].add(flat_values)  72.3 us
    psum x2, blocking collectives, solve_spread(): placed = lax.psum(partial_value, 'col').astype(jnp.bfloat16)  61.2 us
    psum x1, blocking collectives, per_device(): root_solution = lax.psum(root_partial, 'col').astype(jnp.bfloat16)  26.8 us
  transfers between devices with their start and end apart: 5, of which 5 were waited for; matrix products, arithmetic and copies ran while one was open for 6% of the time, Pallas kernels for 0%

commit v1 on v0

v1 whole, which is shorter than its diff:
```python
import functools

import jax
import jax.numpy as jnp
from jax import lax
from jax.experimental import pallas as pl
from jax.experimental.pallas import tpu as pltpu
from jax.sharding import PartitionSpec as P

MESH_ID = pl.DeviceIdType.MESH


def ring_hops(n, plus_longer):
    longer, shorter = n // 2, (n - 1) // 2
    return (longer, shorter) if plus_longer else (shorter, longer)


def arrivals(n):
    plus, minus = ring_hops(n, True)
    order = []
    for k in range(1, plus + 1):
        order.append((1, k))
        if k <= minus:
            order.append((-1, k))
    return order


def gather_kernel(first, second, paired, height, first_stride, second_stride, x_ref, o_ref, *sems):
    first_send, first_recv, second_send, second_recv, own_sem = sems[:5]
    mate_send, mate_recv = sems[5:] if paired else (None, None)
    n_first = lax.axis_size(first) if first else 1
    ways = 2 if paired else 1
    n_second = lax.axis_size(second) // ways
    me_first = lax.axis_index(first) if first else 0
    index = lax.axis_index(second)
    core = lax.rem(index, ways)
    me_second = lax.div(index, ways)
    mate = {second: me_second * ways + 1 - core}

    def first_peer(step):
        return {first: lax.rem(me_first + step + n_first, n_first)}

    def second_peer(step):
        return {second: lax.rem(me_second + step + n_second, n_second) * ways + core}

    def slot(a, b):
        row = pl.multiple_of(a * first_stride + b * second_stride, height)
        return o_ref.at[:, pl.ds(row, height), :]

    def at_first(step):
        return lax.rem(me_first + step + n_first, n_first) if n_first > 1 else me_first

    def at_second(step, side):
        return lax.rem(me_second + step + n_second, n_second) * ways + side

    greet = []
    if n_first > 1:
        greet += [first_peer(1)] + ([first_peer(-1)] if n_first > 2 else [])
    if n_second > 1:
        greet += [second_peer(1)] + ([second_peer(-1)] if n_second > 2 else [])
    if paired:
        greet += [mate]
    barrier = pltpu.get_barrier_semaphore()
    for peer in greet:
        pl.semaphore_signal(barrier, inc=1, device_id=peer, device_id_type=MESH_ID)
    pl.semaphore_wait(barrier, len(greet))

    started = []

    def send(src, dst, send_sem, recv_sem, peer):
        copy = pltpu.make_async_remote_copy(
            src_ref=src,
            dst_ref=dst,
            send_sem=send_sem,
            recv_sem=recv_sem,
            device_id=peer,
            device_id_type=MESH_ID,
        )
        copy.start()
        started.append(copy)

    def arrived(ref, send_sem, recv_sem, peer):
        pltpu.make_async_remote_copy(
            src_ref=ref,
            dst_ref=ref,
            send_sem=send_sem,
            recv_sem=recv_sem,
            device_id=peer,
            device_id_type=MESH_ID,
        ).wait_recv()

    order = arrivals(n_first)
    first_id = {key: i for i, key in enumerate(order)}
    second_id = {}
    for direction in (1, -1):
        for k in range(1, n_second // 2 + 1):
            second_id[direction, k] = len(second_id)
    n_ids = len(second_id)

    own = slot(me_first, index)
    keep = pltpu.make_async_copy(x_ref, own, own_sem)
    keep.start()

    def start_second(j, src, dst):
        hops = ring_hops(n_second, j % 2 == 0)
        for direction, limit in zip((1, -1), hops):
            if limit >= 1:
                i = second_id[direction, 1]
                send(src, dst, second_send.at[j, i], second_recv.at[j, i], second_peer(direction))
        if paired:
            send(src, dst, mate_send.at[j, n_ids], mate_recv.at[j, n_ids], mate)

    plus, minus = ring_hops(n_first, True)
    for direction, limit in ((1, plus), (-1, minus)):
        if limit >= 1:
            i = first_id[direction, 1]
            send(x_ref, own, first_send.at[i], first_recv.at[i], first_peer(direction))
    start_second(0, x_ref, own)

    depth = n_second // 2
    steps = [0] + [-d * k for d, k in order]
    for t in range(1, len(order) + 1 + depth):
        if t <= len(order):
            direction, k = order[t - 1]
            here = slot(at_first(steps[t]), index)
            i = first_id[direction, k]
            arrived(here, first_send.at[i], first_recv.at[i], first_peer(direction))
            if (direction, k + 1) in first_id:
                i = first_id[direction, k + 1]
                send(here, here, first_send.at[i], first_recv.at[i], first_peer(direction))
            start_second(t, here, here)
        for k in range(1, depth + 1):
            j = t - k
            if j < 0 or j > len(order):
                continue
            hops = ring_hops(n_second, j % 2 == 0)
            for direction, limit in zip((1, -1), hops):
                if k > limit:
                    continue
                here = slot(at_first(steps[j]), at_second(-direction * k, core))
                i = second_id[direction, k]
                arrived(here, second_send.at[j, i], second_recv.at[j, i], second_peer(direction))
                if k + 1 <= limit:
                    n = second_id[direction, k + 1]
                    send(
                        here,
                        here,
                        second_send.at[j, n],
                        second_recv.at[j, n],
                        second_peer(direction),
                    )
                if paired:
                    send(here, here, mate_send.at[j, i], mate_recv.at[j, i], mate)
    if paired:
        for j in range(len(order) + 1):
            here = slot(at_first(steps[j]), at_second(0, 1 - core))
            arrived(here, mate_send.at[j, n_ids], mate_recv.at[j, n_ids], mate)
            hops = ring_hops(n_second, j % 2 == 0)
            for direction, limit in zip((1, -1), hops):
                for k in range(1, limit + 1):
                    here = slot(at_first(steps[j]), at_second(-direction * k, 1 - core))
                    i = second_id[direction, k]
                    arrived(here, mate_send.at[j, i], mate_recv.at[j, i], mate)
    for copy in started:
        copy.wait_send()
    keep.wait()


def gather(x, first, second, paired, first_stride, second_stride, collective_id):
    lead, height, width = x.shape
    n_first = lax.axis_size(first) if first else 1
    n_devices = n_first * lax.axis_size(second)
    n_second = lax.axis_size(second) // (2 if paired else 1)
    n_ids = max(2 * (n_second // 2), 1)
    dma = pltpu.SemaphoreType.DMA
    scratch = [dma((max(n_first - 1, 1),))] * 2 + [dma((n_first, n_ids))] * 2 + [dma(())]
    if paired:
        scratch += [dma((n_first, n_ids + 1))] * 2
    body = functools.partial(
        gather_kernel, first, second, paired, height, first_stride, second_stride
    )
    return pl.pallas_call(
        body,
        out_shape=jax.ShapeDtypeStruct((lead, height * n_devices, width), x.dtype),
        in_specs=[pl.BlockSpec(memory_space=pltpu.VMEM)],
        out_specs=pl.BlockSpec(memory_space=pltpu.VMEM),
        scratch_shapes=scratch,
        compiler_params=pltpu.CompilerParams(collective_id=collective_id, has_side_effects=True),
    )(x)


def reduce_kernel(axis, x_ref, o_ref, held, send_sem, recv_sem):
    n = lax.axis_size(axis)
    me = lax.axis_index(axis)
    barrier = pltpu.get_barrier_semaphore()
    for d in range(1, n):
        pl.semaphore_signal(
            barrier, inc=1, device_id={axis: lax.rem(me + d, n)}, device_id_type=MESH_ID
        )
    pl.semaphore_wait(barrier, n - 1)
    copies = []
    for d in range(1, n):
        peer = lax.rem(me + d, n)
        copy = pltpu.make_async_remote_copy(
            src_ref=x_ref.at[peer],
            dst_ref=held.at[d - 1],
            send_sem=send_sem.at[d - 1],
            recv_sem=recv_sem.at[d - 1],
            device_id={axis: peer},
            device_id_type=MESH_ID,
        )
        copy.start()
        copies.append(copy)
    for copy in copies:
        copy.wait()
    total = x_ref[me].astype(jnp.float32)
    for d in range(1, n):
        total = total + held[d - 1].astype(jnp.float32)
    o_ref[...] = total.astype(o_ref.dtype)


def reduce_pieces(x, axis, out_dtype, collective_id):
    n, height, width = x.shape
    return pl.pallas_call(
        functools.partial(reduce_kernel, axis),
        out_shape=jax.ShapeDtypeStruct((height, width), out_dtype),
        in_specs=[pl.BlockSpec(memory_space=pltpu.VMEM)],
        out_specs=pl.BlockSpec(memory_space=pltpu.VMEM),
        scratch_shapes=[
            pltpu.VMEM((n - 1, height, width), x.dtype),
            pltpu.SemaphoreType.DMA((n - 1,)),
            pltpu.SemaphoreType.DMA((n - 1,)),
        ],
        compiler_params=pltpu.CompilerParams(collective_id=collective_id, has_side_effects=True),
    )(x)


def placed_sum(values, rows_list, start, count):
    flat = values.reshape(-1, values.shape[-1])
    offsets = rows_list.reshape(1, -1) - start
    picks = (offsets == lax.broadcasted_iota(jnp.int32, (count, 1), 0)).astype(jnp.bfloat16)
    return jnp.dot(picks, flat, preferred_element_type=jnp.float32)


def per_device(
    child_inverse,
    child_rhs,
    child_to_mid,
    child_to_root,
    mid_rows_list,
    root_rows_list,
    mid_inverse,
    mid_rhs,
    mid_to_root,
    mid_root_list,
    root_inverse,
    root_rhs,
):
    n_row, n_col, n_leaf = (lax.axis_size(name) for name in ("row", "col", "leaf"))
    row, col, leaf = (lax.axis_index(name) for name in ("row", "col", "leaf"))
    children, child_rows = child_inverse.shape[1], child_inverse.shape[2]
    width = child_rhs.shape[3]

    part = jnp.einsum(
        "cij,cjr->cir", child_inverse[0], child_rhs[0], preferred_element_type=jnp.float32
    ).astype(jnp.bfloat16)
    own_rows = child_rows // n_col
    part = part.reshape(children, n_col, own_rows, width).transpose(1, 0, 2, 3)
    solved = reduce_pieces(part.reshape(n_col, children * own_rows, width), "col", jnp.bfloat16, 0)
    child_whole = gather(
        solved.reshape(children, own_rows, width), "row", "col", True, child_rows, own_rows, 1
    )
    child_local = lax.dynamic_slice_in_dim(child_whole, row * child_rows, child_rows, 1)

    update_mid = jnp.einsum(
        "cuj,cjr->cur", child_to_mid[0], child_whole, preferred_element_type=jnp.float32
    ).astype(jnp.bfloat16)
    update_root = jnp.einsum(
        "cuj,cjr->cur", child_to_root[0], child_whole, preferred_element_type=jnp.float32
    ).astype(jnp.bfloat16)
    piece = update_mid.shape[1]
    updates = gather(
        jnp.concatenate((update_mid, update_root), axis=0), "row", "col", True, n_col * piece, piece, 2
    )

    mid_rows = mid_rhs.shape[1]
    mid_term = placed_sum(updates[:children], mid_rows_list, col * mid_rows, mid_rows)
    mid_input = (mid_rhs[0].astype(jnp.float32) - mid_term).astype(jnp.bfloat16)
    mid_part = jnp.dot(mid_inverse[0], mid_input, preferred_element_type=jnp.float32)
    mid_own = mid_inverse.shape[1] // n_col
    mid_solved = reduce_pieces(
        mid_part.astype(jnp.bfloat16).reshape(n_col, mid_own, width), "col", jnp.bfloat16, 3
    )
    mid_block = mid_inverse.shape[1]
    mid_whole = gather(mid_solved[None], "row", "col", True, mid_block, mid_own, 4)[0]
    mid_local = lax.dynamic_slice_in_dim(mid_whole, row * mid_block, mid_block, 0)

    update_top = jnp.dot(
        mid_to_root[0], mid_whole, preferred_element_type=jnp.float32
    ).astype(jnp.bfloat16)
    top_piece = update_top.shape[0]
    top = gather(update_top[None], "row", "col", True, n_col * top_piece, top_piece, 5)

    root_rows = root_rhs.shape[0]
    sub_rows = root_rows // n_row
    start = col * root_rows + row * sub_rows
    root_term = placed_sum(updates[children:], root_rows_list, start, sub_rows)
    root_term = root_term + placed_sum(top, mid_root_list, start, sub_rows)
    root_own = sub_rows // n_leaf
    root_sum = reduce_pieces(
        root_term.reshape(n_leaf, root_own, width), "leaf", jnp.float32, 6
    )
    own_rhs = lax.dynamic_slice_in_dim(root_rhs, row * sub_rows + leaf * root_own, root_own, 0)
    own_input = (own_rhs.astype(jnp.float32) - root_sum).astype(jnp.bfloat16)
    root_input = gather(own_input[None], "leaf", "row", False, root_own, sub_rows, 7)[0]
    root_part = jnp.dot(root_inverse, root_input, preferred_element_type=jnp.float32)
    out_own = root_part.shape[0] // n_col
    root_solved = reduce_pieces(
        root_part.reshape(n_col, out_own, width), "col", jnp.bfloat16, 8
    )
    root_solution = gather(root_solved[None], None, "col", True, 0, out_own, 9)[0]
    return (child_local[None], mid_local[None], root_solution)


def solution(mesh):
    in_specs = (
        P("leaf", None, "row", "col"),
        P("leaf", None, "col", None),
        P("leaf", None, ("row", "col"), None),
        P("leaf", None, ("row", "col"), None),
        P("leaf", None, None),
        P("leaf", None, None),
        P("leaf", "row", "col"),
        P("leaf", "col", None),
        P("leaf", ("row", "col"), None),
        P("leaf", None),
        P(("leaf", "row"), "col"),
        P("col", None),
    )
    out_specs = (P("leaf", None, "row", None), P("leaf", "row", None), P(("leaf", "row"), None))
    return jax.shard_map(
        per_device, mesh=mesh, in_specs=in_specs, out_specs=out_specs, check_vma=False
    )
```

time: 501 us -> 251 us (0.50)
  waiting for transfers between devices: 304 us -> 0 us
  Pallas kernels: 0 us -> 221 us
  blocking collectives: 88 us -> 0 us
  other arithmetic: 74.2 us -> 2 us
  between operations: 14 us -> 0.92 us
    all_gather x4 -> x0, waiting for transfers between devices: 229 us -> none  [the longest x2 141 us: gather_updates(): return lax.all_gather(pieces, ('row', 'col'), axis=2, tiled=True)]
    pallas_call x0 -> x10, Pallas kernels: none -> 221 us  [the longest x6 161 us: gather(): pl.pallas_call(body, out_shape=jax.ShapeDtypeStruct((lead, height * n_dev...]
    psum x3 -> x0, blocking collectives: 88 us -> none  [the longest x2 61.2 us: solve_spread(): placed = lax.psum(partial_value, 'col').astype(jnp.bfloat16)]
    psum x1 -> x0, waiting for transfers between devices: 74.9 us -> none  [per_device(): root_sum = lax.psum(child_root_term + top_term, 'leaf')]
    scatter-add x3 -> x0, other arithmetic: 72.3 us -> none  [scatter_block(): jnp.zeros((piece_rows + 1, width), jnp.float32).at[target].add(flat_values)]
  transfers between devices with their start and end apart: 5 -> 0, of which waited for: 5 -> 0; matrix products, arithmetic and copies ran while one was open for 6% -> 0% of each run, Pallas kernels for 0% -> 0%
where the time goes in v1:
time: 251 us; the launch traced here: 250 us
  Pallas kernels  221 us (88%)
  matrix products  14.5 us (6%)
  local copies, waits for them, and re-layouts  11.8 us (5%)
    pallas_call x6, Pallas kernels, gather(): pl.pallas_call(body, out_shape=jax.ShapeDtypeStruct((lead, height * n_dev...  161 us
    pallas_call x4, Pallas kernels, reduce_pieces(): pl.pallas_call(functools.partial(reduce_kernel, axis), out_shape=jax.Shap...  60 us

profile of v1, /device:TPU:1, one launch (start us, length us, event | category | flops | bytes accessed | tf_op | source)
XLA Modules:
  0.0 250.1 jit_solution(9414107108311942434)
XLA Ops:
  0.6 1.1 copy-done
  1.7 1.4 convolution_convert_fusion
  3.8 17.3 %shard_map.139 = bf16[96,256]{1,0:T(8,128)(2,1)} custom-call(bf16[8,96,256]{2,1,0:T(8,128)(2,1)} %bitcast.80), custom_call_target="tpu_custom_call" | custom-call | tf_op jit(solution)/shard_map/pallas_call | solution.py:224
  21.2 32.2 %shard_map.140 = bf16[2,3072,256]{2,1,0:T(8,128)(2,1)} custom-call(bf16[2,48,256]{2,1,0:T(8,128)(2,1)} %bitcast.86), custom_call_target="tpu_custom_call" | custom-call | tf_op jit(solution)/shard_map/pallas_call | solution.py:182
  53.4 1.9 dynamic-slice_bitcast_fusion
  55.3 2.5 %fusion.9 = bf16[2,32,256]{2,1,0:T(8,128)(2,1)S(1)} fusion(bf16[2,3072,256]{2,1,0:T(8,128)(2,1)} %shard_map.140, bf16[1,2,32,3072]{3,2,1,0:T(8,128)(2,1)S(1)} %copy-done.3), kind=kOutput, calls=%fused_computation.16 | convolution fusion | flops 100679680 | bytes 3571712 | tf_op jit(solution)/shard_map/cuj,cjr->cur/dot_general | solution.py:278
  59.2 34.7 %shard_map.141 = bf16[4,2048,256]{2,1,0:T(8,128)(2,1)} custom-call(bf16[4,32,256]{2,1,0:T(8,128)(2,1)} %pad_maximum_fusion.x_ref), custom_call_target="tpu_custom_call" | custom-call | tf_op jit(solution)/shard_map/pallas_call | solution.py:182
  93.9 3.9 %fusion.30 = (bf16[2,2048,256]{2,1,0:T(8,128)(2,1)}, bf16[2,2048,256]{2,1,0:T(8,128)(2,1)S(1)}) fusion(bf16[4,2048,256]{2,1,0:T(8,128)(2,1)} %shard_map.141), kind=kLoop, calls=%fused_computation.41 | loop fusion | bytes 8388608 | tf_op jit(solution)/shard_map/slice | solution.py:307
  97.8 2.8 %fusion.7 = bf16[512,256]{0,1:T(8,128)(2,1)S(1)} fusion(bf16[4096,256]{1,0:T(8,128)(2,1)S(1)} %bitcast.79, s32[4096]{0:T(1024)S(1)} %bitcast.90, bf16[1,512,512]{2,1,0:T(8,128)(2,1)S(1)} %copy-done.10, bf16[1,512,256]{2,1,0:T(8,128)(2,1)} %param.19), kind=kOutput, calls=%fused_computation.11 | convolution fusion | flops 1210580992 | bytes 3162112 | tf_op jit(solution)/shard_map/dot_general | solution.py:289
  100.6 0.8 copy.16
  101.4 10.1 %shard_map.142 = bf16[64,256]{1,0:T(8,128)(2,1)} custom-call(bf16[8,64,256]{2,1,0:T(8,128)(2,1)} %bitcast.82), custom_call_target="tpu_custom_call" | custom-call | tf_op jit(solution)/shard_map/pallas_call | solution.py:224
  111.6 29.4 %shard_map.143 = bf16[1,4096,256]{2,1,0:T(8,128)(2,1)} custom-call(bf16[1,64,256]{2,1,0:T(8,128)(2,1)} %bitcast.87), custom_call_target="tpu_custom_call" | custom-call | tf_op jit(solution)/shard_map/pallas_call | solution.py:182
  140.9 1.8 constant_dynamic-slice_fusion
  142.8 2.0 fusion.4
  144.9 1.1 fusion.13.x_ref
  145.9 27.3 %shard_map.144 = bf16[1,2048,256]{2,1,0:T(8,128)(2,1)} custom-call(bf16[1,32,256]{2,1,0:T(8,128)(2,1)} %fusion.13.x_ref), custom_call_target="tpu_custom_call" | custom-call | tf_op jit(solution)/shard_map/pallas_call | solution.py:182
  173.3 2.2 convolution_add_fusion
  175.4 14.3 %shard_map.145 = f32[16,256]{1,0:T(8,128)} custom-call(f32[8,16,256]{2,1,0:T(8,128)} %bitcast.83), custom_call_target="tpu_custom_call" | custom-call | tf_op jit(solution)/shard_map/pallas_call | solution.py:224
  189.7 1.3 fusion.29.x_ref
  191.0 27.1 %shard_map.146 = bf16[1,1024,256]{2,1,0:T(8,128)(2,1)} custom-call(bf16[1,16,256]{2,1,0:T(8,128)(2,1)} %fusion.29.x_ref), custom_call_target="tpu_custom_call" | custom-call | tf_op jit(solution)/shard_map/pallas_call | solution.py:182
  218.2 1.9 fusion.20
  220.1 18.2 %shard_map.147 = bf16[16,256]{1,0:T(8,128)(2,1)} custom-call(f32[8,16,256]{2,1,0:T(8,128)} %bitcast.84), custom_call_target="tpu_custom_call" | custom-call | tf_op jit(solution)/shard_map/pallas_call | solution.py:224
  238.3 10.3 %shard_map.148 = bf16[1,128,256]{2,1,0:T(8,128)(2,1)} custom-call(bf16[1,16,256]{2,1,0:T(8,128)(2,1)} %bitcast.89), custom_call_target="tpu_custom_call" | custom-call | tf_op jit(solution)/shard_map/pallas_call | solution.py:182
  248.6 1.5 copy.20
  (29 shorter events, 2.2 us)
Async XLA Ops:
  0.6 1.1 copy-start
  21.2 34.1 %copy-start.3 = (bf16[1,2,32,3072]{3,2,1,0:T(8,128)(2,1)S(1)}, bf16[1,2,32,3072]{3,2,1,0:T(8,128)(2,1)}, u32[]{:S(2)}) copy-start(bf16[1,2,32,3072]{3,2,1,0:T(8,128)(2,1)} %param.15) | copy-start | bytes 1179652
  53.4 4.5 %copy-start.1 = (bf16[2,3072,256]{2,1,0:T(8,128)(2,1)S(1)}, bf16[2,3072,256]{2,1,0:T(8,128)(2,1)}, u32[]{:S(2)}) copy-start(bf16[2,3072,256]{2,1,0:T(8,128)(2,1)} %shard_map.140) | copy-start | bytes 9437188
  53.4 4.5 %copy-start.4 = (bf16[1,2,32,3072]{3,2,1,0:T(8,128)(2,1)S(1)}, bf16[1,2,32,3072]{3,2,1,0:T(8,128)(2,1)}, u32[]{:S(2)}) copy-start(bf16[1,2,32,3072]{3,2,1,0:T(8,128)(2,1)} %param.14) | copy-start | bytes 1179652
  93.8 3.9 %copy-start.7 = (s32[1,2,2048]{2,1,0:T(2,128)S(1)}, s32[1,2,2048]{2,1,0:T(2,128)}, u32[]{:S(2)}) copy-start(s32[1,2,2048]{2,1,0:T(2,128)} %param.16) | copy-start | bytes 49156
  93.8 3.9 %copy-start.10 = (bf16[1,512,512]{2,1,0:T(8,128)(2,1)S(1)}, bf16[1,512,512]{2,1,0:T(8,128)(2,1)}, u32[]{:S(2)}) copy-start(bf16[1,512,512]{2,1,0:T(8,128)(2,1)} %param.18) | copy-start | bytes 1572868
  100.6 42.2 %copy-start.8 = (s32[1,2,2048]{2,1,0:T(2,128)S(1)}, s32[1,2,2048]{2,1,0:T(2,128)}, u32[]{:S(2)}) copy-start(s32[1,2,2048]{2,1,0:T(2,128)} %param.17) | copy-start | bytes 49156
  111.5 33.3 %copy-start.5 = (bf16[1,32,4096]{2,1,0:T(8,128)(2,1)S(1)}, bf16[1,32,4096]{2,1,0:T(8,128)(2,1)}, u32[]{:S(2)}) copy-start(bf16[1,32,4096]{2,1,0:T(8,128)(2,1)} %param.20) | copy-start | bytes 786436
  140.9 3.9 %copy-start.2 = (bf16[1,4096,256]{2,1,0:T(8,128)(2,1)S(1)}, bf16[1,4096,256]{2,1,0:T(8,128)(2,1)}, u32[]{:S(2)}) copy-start(bf16[1,4096,256]{2,1,0:T(8,128)(2,1)} %shard_map.143) | copy-start | bytes 6291460
  144.8 28.4 %copy-start.9 = (s32[1,2048]{1,0:T(1,128)S(1)}, s32[1,2048]{1,0:T(1,128)}, u32[]{:S(2)}) copy-start(s32[1,2048]{1,0:T(1,128)} %param.21) | copy-start | bytes 24580
  145.9 72.2 %copy-start.6 = (bf16[128,1024]{1,0:T(8,128)(2,1)S(1)}, bf16[128,1024]{1,0:T(8,128)(2,1)}, u32[]{:S(2)}) copy-start(bf16[128,1024]{1,0:T(8,128)(2,1)} %param.22) | copy-start | bytes 786436

commit v2 on v0

v2 whole, which is shorter than its diff:
```python
import functools

import jax
import jax.numpy as jnp
from jax import lax
from jax.experimental import pallas as pl
from jax.experimental.pallas import tpu as pltpu
from jax.sharding import PartitionSpec as P

MESH_ID = pl.DeviceIdType.MESH


def ring_hops(n, plus_longer):
    longer, shorter = n // 2, (n - 1) // 2
    return (longer, shorter) if plus_longer else (shorter, longer)


def spread_kernel(reduced, negated, first, second, paired, first_stride, second_stride, *refs):
    x_ref = refs[0]
    base_ref = refs[1] if negated else None
    o_ref = refs[1 + negated]
    scratch = refs[2 + negated :]
    first_send, first_recv, second_send, second_recv, mate_send, mate_recv, own_sem = scratch[:7]
    lead, height, width = x_ref.shape[-3:]
    n_first = lax.axis_size(first) if first else 1
    ways = 2 if paired else 1
    n_second = lax.axis_size(second) // ways
    relayed = n_second <= 4
    me_first = lax.axis_index(first) if first else 0
    index = lax.axis_index(second)
    core = lax.rem(index, ways)
    chip = lax.div(index, ways)
    mate = {second: chip * ways + 1 - core}

    def at_first(step):
        return lax.rem(me_first + step + n_first, n_first) if n_first > 1 else me_first

    def at_second(step, side):
        return lax.rem(chip + step + n_second, n_second) * ways + side

    def slot(a, b):
        row = pl.multiple_of(a * first_stride + b * second_stride, height)
        return o_ref.at[:, pl.ds(row, height), :]

    started = []

    def make(src, dst, send_sem, recv_sem, peer):
        return pltpu.make_async_remote_copy(
            src_ref=src,
            dst_ref=dst,
            send_sem=send_sem,
            recv_sem=recv_sem,
            device_id=peer,
            device_id_type=MESH_ID,
        )

    def send(*args):
        copy = make(*args)
        copy.start()
        started.append(copy)

    def arrived(ref, send_sem, recv_sem, peer):
        make(ref, ref, send_sem, recv_sem, peer).wait_recv()

    n_reduced = lax.axis_size(reduced) if reduced else 1
    me_reduced = lax.axis_index(reduced) if reduced else 0
    reduce_peers = [{reduced: lax.rem(me_reduced + d, n_reduced)} for d in range(1, n_reduced)]
    greet = list(reduce_peers)
    if reduced != first:
        greet += [{first: at_first(d)} for d in range(1, n_first)]
    if reduced != second:
        greet += [{second: at_second(d, core)} for d in range(1, n_second)]
        greet += [mate] if paired else []
    barrier = pltpu.get_barrier_semaphore()
    for peer in greet:
        pl.semaphore_signal(barrier, inc=1, device_id=peer, device_id_type=MESH_ID)
    pl.semaphore_wait(barrier, len(greet))

    own = slot(me_first, index)
    if reduced:
        held, reduce_send, reduce_recv = scratch[7:]
        pieces = []
        for d in sorted(range(1, n_reduced), key=lambda d: -min(d, n_reduced - d)):
            copy = make(
                x_ref.at[lax.rem(me_reduced + d, n_reduced)],
                held.at[d - 1],
                reduce_send.at[d - 1],
                reduce_recv.at[d - 1],
                reduce_peers[d - 1],
            )
            copy.start()
            pieces.append(copy)
        total = x_ref[me_reduced].astype(jnp.float32)
        for copy in pieces:
            copy.wait_recv()
        for d in range(1, n_reduced):
            total = total + held[d - 1].astype(jnp.float32)
        if negated:
            total = base_ref[...].astype(jnp.float32) - total
        own_row = pl.multiple_of(me_first * first_stride + index * second_stride, height)
        o_ref[:, pl.ds(own_row, height), :] = total.astype(o_ref.dtype)
        started.extend(pieces)
        src = own
    else:
        keep = pltpu.make_async_copy(x_ref, own, own_sem)
        keep.start()
        src = x_ref

    order = sorted(range(1, n_first), key=lambda d: min(d, n_first - d))
    for d in order:
        send(src, own, first_send.at[d - 1], first_recv.at[d - 1], {first: at_first(d)})

    far_first = sorted(range(1, n_second), key=lambda d: -min(d, n_second - d))

    def start_second(j, src, dst):
        if relayed:
            for direction, limit in zip((1, -1), ring_hops(n_second, j % 2 == 0)):
                if limit >= 1:
                    e = direction % n_second - 1
                    peer = {second: at_second(direction, core)}
                    send(src, dst, second_send.at[j, e], second_recv.at[j, e], peer)
        else:
            for d in far_first:
                peer = {second: at_second(d, core)}
                send(src, dst, second_send.at[j, d - 1], second_recv.at[j, d - 1], peer)
        if paired:
            send(src, dst, mate_send.at[j, 0], mate_recv.at[j, 0], mate)

    steps = [0] + order

    def take_second(j, direction, k, limit):
        d = direction * k % n_second
        here = slot(at_first(-steps[j]), at_second(-d, core))
        hop = direction if relayed else d
        peer = {second: at_second(hop, core)}
        arrived(here, second_send.at[j, d - 1], second_recv.at[j, d - 1], peer)
        if k + 1 <= limit:
            e = direction * (k + 1) % n_second - 1
            send(here, here, second_send.at[j, e], second_recv.at[j, e], peer)
        if paired:
            send(here, here, mate_send.at[j, d], mate_recv.at[j, d], mate)

    start_second(0, src, own)
    depth = n_second // 2 if relayed else 1
    lag = 1
    for t in range(1, n_first + lag + depth):
        if t < n_first:
            d = steps[t]
            here = slot(at_first(-d), index)
            arrived(here, first_send.at[d - 1], first_recv.at[d - 1], {first: at_first(d)})
            start_second(t, here, here)
        for k in range(1, depth + 1):
            j = t - lag - k + 1
            if j < 0 or j >= n_first:
                continue
            if relayed:
                for direction, limit in zip((1, -1), ring_hops(n_second, j % 2 == 0)):
                    if k <= limit:
                        take_second(j, direction, k, limit)
            else:
                for d in far_first[::-1]:
                    take_second(j, d, 1, 1)
    if paired:
        for j in range(n_first):
            for d in range(n_second):
                here = slot(at_first(-steps[j]), at_second(-d, 1 - core))
                arrived(here, mate_send.at[j, d], mate_recv.at[j, d], mate)
    for copy in started:
        copy.wait_send()
    if not reduced:
        keep.wait()


def spread(x, reduced, first, second, paired, first_stride, second_stride, collective_id, base=None):
    lead, height, width = x.shape[-3:]
    n_first = lax.axis_size(first) if first else 1
    n_devices = n_first * lax.axis_size(second)
    n_second = lax.axis_size(second) // (2 if paired else 1)
    dma = pltpu.SemaphoreType.DMA
    scratch = [dma((max(n_first - 1, 1),))] * 2 + [dma((n_first, max(n_second - 1, 1)))] * 2
    scratch += [dma((n_first, n_second))] * 2 + [dma(())]
    if reduced:
        n = x.shape[0] - 1
        scratch += [pltpu.VMEM((n,) + x.shape[1:], x.dtype), dma((n,)), dma((n,))]
    operands = (x,) if base is None else (x, base)
    body = functools.partial(
        spread_kernel, reduced, base is not None, first, second, paired, first_stride, second_stride
    )
    return pl.pallas_call(
        body,
        out_shape=jax.ShapeDtypeStruct((lead, height * n_devices, width), jnp.bfloat16),
        in_specs=[pl.BlockSpec(memory_space=pltpu.VMEM)] * len(operands),
        out_specs=pl.BlockSpec(memory_space=pltpu.VMEM),
        scratch_shapes=scratch,
        compiler_params=pltpu.CompilerParams(collective_id=collective_id, has_side_effects=True),
    )(*operands)


def placed_sum(values, rows_list, start, count):
    flat = values.reshape(-1, values.shape[-1])
    offsets = rows_list.reshape(1, -1) - start
    picks = (offsets == lax.broadcasted_iota(jnp.int32, (count, 1), 0)).astype(jnp.bfloat16)
    return jnp.dot(picks, flat, preferred_element_type=jnp.float32)


def per_device(
    child_inverse,
    child_rhs,
    child_to_mid,
    child_to_root,
    mid_rows_list,
    root_rows_list,
    mid_inverse,
    mid_rhs,
    mid_to_root,
    mid_root_list,
    root_inverse,
    root_rhs,
):
    n_row, n_col, n_leaf = (lax.axis_size(name) for name in ("row", "col", "leaf"))
    row, col, leaf = (lax.axis_index(name) for name in ("row", "col", "leaf"))
    children, child_rows = child_inverse.shape[1], child_inverse.shape[2]
    width = child_rhs.shape[3]

    part = jnp.einsum(
        "cij,cjr->cir", child_inverse[0], child_rhs[0], preferred_element_type=jnp.float32
    ).astype(jnp.bfloat16)
    own_rows = child_rows // n_col
    part = part.reshape(children, n_col, own_rows, width).transpose(1, 0, 2, 3)
    child_whole = spread(part, "col", "row", "col", True, child_rows, own_rows, 0)
    child_local = lax.dynamic_slice_in_dim(child_whole, row * child_rows, child_rows, 1)

    update_mid = jnp.einsum(
        "cuj,cjr->cur", child_to_mid[0], child_whole, preferred_element_type=jnp.float32
    ).astype(jnp.bfloat16)
    update_root = jnp.einsum(
        "cuj,cjr->cur", child_to_root[0], child_whole, preferred_element_type=jnp.float32
    ).astype(jnp.bfloat16)
    piece = update_mid.shape[1]
    stacked = jnp.concatenate((update_mid, update_root), axis=0)
    updates = spread(stacked, None, "row", "col", True, n_col * piece, piece, 1)

    mid_rows = mid_rhs.shape[1]
    mid_term = placed_sum(updates[:children], mid_rows_list, col * mid_rows, mid_rows)
    mid_input = (mid_rhs[0].astype(jnp.float32) - mid_term).astype(jnp.bfloat16)
    mid_part = jnp.dot(mid_inverse[0], mid_input, preferred_element_type=jnp.float32)
    mid_own = mid_inverse.shape[1] // n_col
    mid_block = mid_inverse.shape[1]
    mid_part = mid_part.astype(jnp.bfloat16).reshape(n_col, 1, mid_own, width)
    mid_whole = spread(mid_part, "col", "row", "col", True, mid_block, mid_own, 2)[0]
    mid_local = lax.dynamic_slice_in_dim(mid_whole, row * mid_block, mid_block, 0)

    update_top = jnp.dot(
        mid_to_root[0], mid_whole, preferred_element_type=jnp.float32
    ).astype(jnp.bfloat16)
    top_piece = update_top.shape[0]
    top = spread(update_top[None], None, "row", "col", True, n_col * top_piece, top_piece, 3)

    root_rows = root_rhs.shape[0]
    sub_rows = root_rows // n_row
    start = col * root_rows + row * sub_rows
    root_term = placed_sum(updates[children:], root_rows_list, start, sub_rows)
    root_term = root_term + placed_sum(top, mid_root_list, start, sub_rows)
    root_own = sub_rows // n_leaf
    own_rhs = lax.dynamic_slice_in_dim(root_rhs, row * sub_rows + leaf * root_own, root_own, 0)
    root_term = root_term.reshape(n_leaf, 1, root_own, width)
    root_input = spread(
        root_term, "leaf", "leaf", "row", False, root_own, sub_rows, 4, own_rhs[None]
    )[0]
    root_part = jnp.dot(root_inverse, root_input, preferred_element_type=jnp.float32)
    out_own = root_part.shape[0] // n_col
    root_part = root_part.reshape(n_col, 1, out_own, width)
    root_solution = spread(root_part, "col", None, "col", True, 0, out_own, 5)[0]
    return (child_local[None], mid_local[None], root_solution)


def solution(mesh):
    in_specs = (
        P("leaf", None, "row", "col"),
        P("leaf", None, "col", None),
        P("leaf", None, ("row", "col"), None),
        P("leaf", None, ("row", "col"), None),
        P("leaf", None, None),
        P("leaf", None, None),
        P("leaf", "row", "col"),
        P("leaf", "col", None),
        P("leaf", ("row", "col"), None),
        P("leaf", None),
        P(("leaf", "row"), "col"),
        P("col", None),
    )
    out_specs = (P("leaf", None, "row", None), P("leaf", "row", None), P(("leaf", "row"), None))
    return jax.shard_map(
        per_device, mesh=mesh, in_specs=in_specs, out_specs=out_specs, check_vma=False
    )
```

time: 501 us -> 237 us (0.47)
  waiting for transfers between devices: 304 us -> 0 us
  Pallas kernels: 0 us -> 207 us
  blocking collectives: 88 us -> 0 us
  other arithmetic: 74.2 us -> 0.67 us
  between operations: 14 us -> 0.88 us
  local copies, waits for them, and re-layouts: 7.04 us -> 13.1 us
    all_gather x4 -> x0, waiting for transfers between devices: 229 us -> none  [the longest x2 141 us: gather_updates(): return lax.all_gather(pieces, ('row', 'col'), axis=2, tiled=True)]
    pallas_call x0 -> x6, Pallas kernels: none -> 207 us  [spread(): pl.pallas_call(body, out_shape=jax.ShapeDtypeStruct((lead, height * n_dev...]
    psum x3 -> x0, blocking collectives: 88 us -> none  [the longest x2 61.2 us: solve_spread(): placed = lax.psum(partial_value, 'col').astype(jnp.bfloat16)]
    psum x1 -> x0, waiting for transfers between devices: 74.9 us -> none  [per_device(): root_sum = lax.psum(child_root_term + top_term, 'leaf')]
    scatter-add x3 -> x0, other arithmetic: 72.3 us -> none  [scatter_block(): jnp.zeros((piece_rows + 1, width), jnp.float32).at[target].add(flat_values)]
  transfers between devices with their start and end apart: 5 -> 0, of which waited for: 5 -> 0; matrix products, arithmetic and copies ran while one was open for 6% -> 0% of each run, Pallas kernels for 0% -> 0%
where the time goes in v2:
time: 237 us; the launch traced here: 236 us
  Pallas kernels  207 us (87%)
  matrix products  14.5 us (6%)
  local copies, waits for them, and re-layouts  13.1 us (6%)
    pallas_call x6, Pallas kernels, spread(): pl.pallas_call(body, out_shape=jax.ShapeDtypeStruct((lead, height * n_dev...  207 us

profile of v2, /device:TPU:1, one launch (start us, length us, event | category | flops | bytes accessed | tf_op | source)
XLA Modules:
  0.0 236.2 jit_solution(5039071542634660350)
XLA Ops:
  0.6 1.1 copy-done
  1.7 1.4 convolution_convert_fusion
  3.1 0.8 copy.21
  3.8 44.6 %shard_map.139 = bf16[2,3072,256]{2,1,0:T(8,128)(2,1)} custom-call(bf16[8,2,48,256]{3,2,1,0:T(8,128)(2,1)} %bitcast.77), custom_call_target="tpu_custom_call" | custom-call | tf_op jit(solution)/shard_map/pallas_call | solution.py:189
  48.5 1.9 dynamic-slice_bitcast_fusion
  50.4 2.5 %fusion.9 = bf16[2,32,256]{2,1,0:T(8,128)(2,1)S(1)} fusion(bf16[2,3072,256]{2,1,0:T(8,128)(2,1)} %shard_map.139, bf16[1,2,32,3072]{3,2,1,0:T(8,128)(2,1)S(1)} %copy-done.3), kind=kOutput, calls=%fused_computation.16 | convolution fusion | flops 100679680 | bytes 3571712 | tf_op jit(solution)/shard_map/cuj,cjr->cur/dot_general | solution.py:236
  53.0 0.0 copy-done.1
  53.0 0.6 fusion.8
  53.6 0.6 pad_maximum_fusion.refs_0_
  54.3 36.7 %shard_map.140 = bf16[4,2048,256]{2,1,0:T(8,128)(2,1)} custom-call(bf16[4,32,256]{2,1,0:T(8,128)(2,1)} %pad_maximum_fusion.refs_0_), custom_call_target="tpu_custom_call" | custom-call | tf_op jit(solution)/shard_map/pallas_call | solution.py:189
  91.0 3.9 %fusion.29 = (bf16[2,2048,256]{2,1,0:T(8,128)(2,1)}, bf16[2,2048,256]{2,1,0:T(8,128)(2,1)S(1)}) fusion(bf16[4,2048,256]{2,1,0:T(8,128)(2,1)} %shard_map.140), kind=kLoop, calls=%fused_computation.41 | loop fusion | bytes 8388608 | tf_op jit(solution)/shard_map/slice | solution.py:262
  95.0 2.8 %fusion.7 = bf16[512,256]{0,1:T(8,128)(2,1)S(1)} fusion(bf16[4096,256]{1,0:T(8,128)(2,1)S(1)} %bitcast.76, s32[4096]{0:T(1024)S(1)} %bitcast.84, bf16[1,512,512]{2,1,0:T(8,128)(2,1)S(1)} %copy-done.10, bf16[1,512,256]{2,1,0:T(8,128)(2,1)} %param.19), kind=kOutput, calls=%fused_computation.11 | convolution fusion | flops 1210580992 | bytes 3162112 | tf_op jit(solution)/shard_map/dot_general | solution.py:246
  97.8 0.8 copy.17
  98.6 37.7 %shard_map.141 = bf16[1,4096,256]{2,1,0:T(8,128)(2,1)} custom-call(bf16[8,1,64,256]{3,2,1,0:T(8,128)(2,1)} %bitcast.79), custom_call_target="tpu_custom_call" | custom-call | tf_op jit(solution)/shard_map/pallas_call | solution.py:189
  136.4 1.8 constant_dynamic-slice_fusion
  138.2 2.0 fusion.4
  140.3 1.1 fusion.13.refs_0_
  141.4 29.4 %shard_map.142 = bf16[1,2048,256]{2,1,0:T(8,128)(2,1)} custom-call(bf16[1,32,256]{2,1,0:T(8,128)(2,1)} %fusion.13.refs_0_), custom_call_target="tpu_custom_call" | custom-call | tf_op jit(solution)/shard_map/pallas_call | solution.py:189
  170.8 2.2 convolution_add_fusion
  173.0 1.3 dynamic-slice_bitcast_fusion.1.refs_1_
  174.3 37.9 %shard_map.143 = bf16[1,1024,256]{2,1,0:T(8,128)(2,1)} custom-call(f32[8,1,16,256]{3,2,1,0:T(8,128)} %bitcast.81, bf16[1,16,256]{2,1,0:T(8,128)(2,1)} %dynamic-slice_bitcast_fusion.1.refs_1_), custom_call_target="tpu_custom_call" | custom-call | tf_op jit(solution)/shard_map/pallas_call | solution.py:189
  212.2 1.9 fusion.20
  214.1 20.6 %shard_map.144 = bf16[1,128,256]{2,1,0:T(8,128)(2,1)} custom-call(f32[8,1,16,256]{3,2,1,0:T(8,128)} %bitcast.80), custom_call_target="tpu_custom_call" | custom-call | tf_op jit(solution)/shard_map/pallas_call | solution.py:189
  234.7 1.5 copy.23
  (25 shorter events, 0.1 us)
Async XLA Ops:
  0.6 1.1 copy-start
  3.8 46.6 %copy-start.3 = (bf16[1,2,32,3072]{3,2,1,0:T(8,128)(2,1)S(1)}, bf16[1,2,32,3072]{3,2,1,0:T(8,128)(2,1)}, u32[]{:S(2)}) copy-start(bf16[1,2,32,3072]{3,2,1,0:T(8,128)(2,1)} %param.15) | copy-start | bytes 1179652
  48.5 4.5 %copy-start.1 = (bf16[2,3072,256]{2,1,0:T(8,128)(2,1)S(1)}, bf16[2,3072,256]{2,1,0:T(8,128)(2,1)}, u32[]{:S(2)}) copy-start(bf16[2,3072,256]{2,1,0:T(8,128)(2,1)} %shard_map.139) | copy-start | bytes 9437188
  48.5 4.5 %copy-start.4 = (bf16[1,2,32,3072]{3,2,1,0:T(8,128)(2,1)S(1)}, bf16[1,2,32,3072]{3,2,1,0:T(8,128)(2,1)}, u32[]{:S(2)}) copy-start(bf16[1,2,32,3072]{3,2,1,0:T(8,128)(2,1)} %param.14) | copy-start | bytes 1179652
  91.0 3.9 %copy-start.7 = (s32[1,2,2048]{2,1,0:T(2,128)S(1)}, s32[1,2,2048]{2,1,0:T(2,128)}, u32[]{:S(2)}) copy-start(s32[1,2,2048]{2,1,0:T(2,128)} %param.16) | copy-start | bytes 49156
  91.0 3.9 %copy-start.10 = (bf16[1,512,512]{2,1,0:T(8,128)(2,1)S(1)}, bf16[1,512,512]{2,1,0:T(8,128)(2,1)}, u32[]{:S(2)}) copy-start(bf16[1,512,512]{2,1,0:T(8,128)(2,1)} %param.18) | copy-start | bytes 1572868
  97.7 40.5 %copy-start.8 = (s32[1,2,2048]{2,1,0:T(2,128)S(1)}, s32[1,2,2048]{2,1,0:T(2,128)}, u32[]{:S(2)}) copy-start(s32[1,2,2048]{2,1,0:T(2,128)} %param.17) | copy-start | bytes 49156
  136.3 3.9 %copy-start.2 = (bf16[1,4096,256]{2,1,0:T(8,128)(2,1)S(1)}, bf16[1,4096,256]{2,1,0:T(8,128)(2,1)}, u32[]{:S(2)}) copy-start(bf16[1,4096,256]{2,1,0:T(8,128)(2,1)} %shard_map.141) | copy-start | bytes 6291460
  136.4 3.9 %copy-start.5 = (bf16[1,32,4096]{2,1,0:T(8,128)(2,1)S(1)}, bf16[1,32,4096]{2,1,0:T(8,128)(2,1)}, u32[]{:S(2)}) copy-start(bf16[1,32,4096]{2,1,0:T(8,128)(2,1)} %param.20) | copy-start | bytes 786436
  140.3 30.5 %copy-start.9 = (s32[1,2048]{1,0:T(1,128)S(1)}, s32[1,2048]{1,0:T(1,128)}, u32[]{:S(2)}) copy-start(s32[1,2048]{1,0:T(1,128)} %param.21) | copy-start | bytes 24580
  141.4 70.8 %copy-start.6 = (bf16[128,1024]{1,0:T(8,128)(2,1)S(1)}, bf16[128,1024]{1,0:T(8,128)(2,1)}, u32[]{:S(2)}) copy-start(bf16[128,1024]{1,0:T(8,128)(2,1)} %param.22) | copy-start | bytes 786436

commit v3 on v2

--- a/solution.py
+++ b/solution.py
@@ -8,6 +8,7 @@
 from jax.sharding import PartitionSpec as P
 
 MESH_ID = pl.DeviceIdType.MESH
+RELAY = False
 
 
 def ring_hops(n, plus_longer):
@@ -25,7 +26,7 @@
     n_first = lax.axis_size(first) if first else 1
     ways = 2 if paired else 1
     n_second = lax.axis_size(second) // ways
-    relayed = n_second <= 4
+    relayed = RELAY and n_second <= 4
     me_first = lax.axis_index(first) if first else 0
     index = lax.axis_index(second)
     core = lax.rem(index, ways)
@@ -141,25 +142,21 @@
             send(here, here, mate_send.at[j, d], mate_recv.at[j, d], mate)
 
     start_second(0, src, own)
-    depth = n_second // 2 if relayed else 1
-    lag = 1
-    for t in range(1, n_first + lag + depth):
-        if t < n_first:
-            d = steps[t]
-            here = slot(at_first(-d), index)
-            arrived(here, first_send.at[d - 1], first_recv.at[d - 1], {first: at_first(d)})
-            start_second(t, here, here)
-        for k in range(1, depth + 1):
-            j = t - lag - k + 1
-            if j < 0 or j >= n_first:
-                continue
-            if relayed:
+    for j in range(1, n_first):
+        d = steps[j]
+        here = slot(at_first(-d), index)
+        arrived(here, first_send.at[d - 1], first_recv.at[d - 1], {first: at_first(d)})
+        start_second(j, here, here)
+    if relayed:
+        for k in range(1, n_second // 2 + 1):
+            for j in range(n_first):
                 for direction, limit in zip((1, -1), ring_hops(n_second, j % 2 == 0)):
                     if k <= limit:
                         take_second(j, direction, k, limit)
-            else:
-                for d in far_first[::-1]:
-                    take_second(j, d, 1, 1)
+    else:
+        for j in range(n_first):
+            for d in far_first[::-1]:
+                take_second(j, d, 1, 1)
     if paired:
         for j in range(n_first):
             for d in range(n_second):
@@ -265,7 +262,7 @@
     own_rhs = lax.dynamic_slice_in_dim(root_rhs, row * sub_rows + leaf * root_own, root_own, 0)
     root_term = root_term.reshape(n_leaf, 1, root_own, width)
     root_input = spread(
-        root_term, "leaf", "leaf", "row", False, root_own, sub_rows, 4, own_rhs[None]
+        root_term, "leaf", "row", "leaf", False, sub_rows, root_own, 4, own_rhs[None]
     )[0]
     root_part = jnp.dot(root_inverse, root_input, preferred_element_type=jnp.float32)
     out_own = root_part.shape[0] // n_col

time: 237 us -> 197 us (0.83)
  Pallas kernels: 207 us -> 167 us
    pallas_call x6, Pallas kernels: 207 us -> 167 us  [spread(): pl.pallas_call(body, out_shape=jax.ShapeDtypeStruct((lead, height * n_dev...]
where the time goes in v3:
time: 197 us; the launch traced here: 196 us
  Pallas kernels  167 us (85%)
  matrix products  14.5 us (7%)
  local copies, waits for them, and re-layouts  13.1 us (7%)
    pallas_call x6, Pallas kernels, spread(): pl.pallas_call(body, out_shape=jax.ShapeDtypeStruct((lead, height * n_dev...  167 us
    dot_general x2, matrix products, placed_sum(): return jnp.dot(picks, flat, preferred_element_type=jnp.float32)  4.2 us

profile of v3, /device:TPU:1, one launch (start us, length us, event | category | flops | bytes accessed | tf_op | source)
XLA Modules:
  0.0 196.4 jit_solution(3148716102506927335)
XLA Ops:
  0.6 1.1 copy-done
  1.7 1.4 convolution_convert_fusion
  3.1 0.8 copy.21
  3.8 39.5 %shard_map.139 = bf16[2,3072,256]{2,1,0:T(8,128)(2,1)} custom-call(bf16[8,2,48,256]{3,2,1,0:T(8,128)(2,1)} %bitcast.77), custom_call_target="tpu_custom_call" | custom-call | tf_op jit(solution)/shard_map/pallas_call | solution.py:186
  43.4 1.9 dynamic-slice_bitcast_fusion
  45.3 2.5 %fusion.9 = bf16[2,32,256]{2,1,0:T(8,128)(2,1)S(1)} fusion(bf16[2,3072,256]{2,1,0:T(8,128)(2,1)} %shard_map.139, bf16[1,2,32,3072]{3,2,1,0:T(8,128)(2,1)S(1)} %copy-done.3), kind=kOutput, calls=%fused_computation.16 | convolution fusion | flops 100679680 | bytes 3571712 | tf_op jit(solution)/shard_map/cuj,cjr->cur/dot_general | solution.py:233
  47.8 0.0 copy-done.1
  47.8 0.6 fusion.8
  48.5 0.6 pad_maximum_fusion.refs_0_
  49.1 34.0 %shard_map.140 = bf16[4,2048,256]{2,1,0:T(8,128)(2,1)} custom-call(bf16[4,32,256]{2,1,0:T(8,128)(2,1)} %pad_maximum_fusion.refs_0_), custom_call_target="tpu_custom_call" | custom-call | tf_op jit(solution)/shard_map/pallas_call | solution.py:186
  83.2 3.9 %fusion.29 = (bf16[2,2048,256]{2,1,0:T(8,128)(2,1)}, bf16[2,2048,256]{2,1,0:T(8,128)(2,1)S(1)}) fusion(bf16[4,2048,256]{2,1,0:T(8,128)(2,1)} %shard_map.140), kind=kLoop, calls=%fused_computation.41 | loop fusion | bytes 8388608 | tf_op jit(solution)/shard_map/slice | solution.py:259
  87.1 2.8 %fusion.7 = bf16[512,256]{0,1:T(8,128)(2,1)S(1)} fusion(bf16[4096,256]{1,0:T(8,128)(2,1)S(1)} %bitcast.76, s32[4096]{0:T(1024)S(1)} %bitcast.84, bf16[1,512,512]{2,1,0:T(8,128)(2,1)S(1)} %copy-done.10, bf16[1,512,256]{2,1,0:T(8,128)(2,1)} %param.19), kind=kOutput, calls=%fused_computation.11 | convolution fusion | flops 1210580992 | bytes 3162112 | tf_op jit(solution)/shard_map/dot_general | solution.py:243
  89.9 0.8 copy.17
  90.7 28.6 %shard_map.141 = bf16[1,4096,256]{2,1,0:T(8,128)(2,1)} custom-call(bf16[8,1,64,256]{3,2,1,0:T(8,128)(2,1)} %bitcast.79), custom_call_target="tpu_custom_call" | custom-call | tf_op jit(solution)/shard_map/pallas_call | solution.py:186
  119.4 1.8 constant_dynamic-slice_fusion
  121.2 2.0 %fusion.4 = f32[128,256]{1,0:T(8,128)S(1)} fusion(bf16[4096,256]{1,0:T(8,128)(2,1)} %bitcast.75, s32[4096]{0:T(1024)S(1)} %bitcast.85), kind=kOutput, calls=%fused_computation.6 | convolution fusion | flops 268959744 | bytes 2244608 | tf_op jit(solution)/shard_map/dot_general | solution.py:200
  123.3 1.1 fusion.13.refs_0_
  124.4 17.8 %shard_map.142 = bf16[1,2048,256]{2,1,0:T(8,128)(2,1)} custom-call(bf16[1,32,256]{2,1,0:T(8,128)(2,1)} %fusion.13.refs_0_), custom_call_target="tpu_custom_call" | custom-call | tf_op jit(solution)/shard_map/pallas_call | solution.py:186
  142.2 2.2 %convolution_add_fusion = f32[128,256]{1,0:T(8,128)} fusion(f32[128,256]{1,0:T(8,128)S(1)} %fusion.4, bf16[1,2048,256]{2,1,0:T(8,128)(2,1)} %shard_map.142, s32[2048]{0:T(1024)S(1)} %bitcast.83), kind=kOutput, calls=%fused_computation.12 | convolution fusion | flops 134512640 | bytes 1318912 | tf_op jit(solution)/shard_map/dot_general | solution.py:200
  144.4 1.3 dynamic-slice_bitcast_fusion.1.refs_1_
  145.7 33.2 %shard_map.143 = bf16[1,1024,256]{2,1,0:T(8,128)(2,1)} custom-call(f32[8,1,16,256]{3,2,1,0:T(8,128)} %bitcast.81, bf16[1,16,256]{2,1,0:T(8,128)(2,1)} %dynamic-slice_bitcast_fusion.1.refs_1_), custom_call_target="tpu_custom_call" | custom-call | tf_op jit(solution)/shard_map/pallas_call | solution.py:186
  178.9 1.9 fusion.20
  180.8 14.1 %shard_map.144 = bf16[1,128,256]{2,1,0:T(8,128)(2,1)} custom-call(f32[8,1,16,256]{3,2,1,0:T(8,128)} %bitcast.80), custom_call_target="tpu_custom_call" | custom-call | tf_op jit(solution)/shard_map/pallas_call | solution.py:186
  194.9 1.5 copy.23
  (25 shorter events, 0.1 us)
Async XLA Ops:
  0.6 1.1 copy-start
  3.8 41.4 %copy-start.3 = (bf16[1,2,32,3072]{3,2,1,0:T(8,128)(2,1)S(1)}, bf16[1,2,32,3072]{3,2,1,0:T(8,128)(2,1)}, u32[]{:S(2)}) copy-start(bf16[1,2,32,3072]{3,2,1,0:T(8,128)(2,1)} %param.15) | copy-start | bytes 1179652
  43.3 4.5 %copy-start.1 = (bf16[2,3072,256]{2,1,0:T(8,128)(2,1)S(1)}, bf16[2,3072,256]{2,1,0:T(8,128)(2,1)}, u32[]{:S(2)}) copy-start(bf16[2,3072,256]{2,1,0:T(8,128)(2,1)} %shard_map.139) | copy-start | bytes 9437188
  43.3 4.5 %copy-start.4 = (bf16[1,2,32,3072]{3,2,1,0:T(8,128)(2,1)S(1)}, bf16[1,2,32,3072]{3,2,1,0:T(8,128)(2,1)}, u32[]{:S(2)}) copy-start(bf16[1,2,32,3072]{3,2,1,0:T(8,128)(2,1)} %param.14) | copy-start | bytes 1179652
  83.1 3.9 %copy-start.7 = (s32[1,2,2048]{2,1,0:T(2,128)S(1)}, s32[1,2,2048]{2,1,0:T(2,128)}, u32[]{:S(2)}) copy-start(s32[1,2,2048]{2,1,0:T(2,128)} %param.16) | copy-start | bytes 49156
  83.2 3.9 %copy-start.10 = (bf16[1,512,512]{2,1,0:T(8,128)(2,1)S(1)}, bf16[1,512,512]{2,1,0:T(8,128)(2,1)}, u32[]{:S(2)}) copy-start(bf16[1,512,512]{2,1,0:T(8,128)(2,1)} %param.18) | copy-start | bytes 1572868
  89.9 31.3 %copy-start.8 = (s32[1,2,2048]{2,1,0:T(2,128)S(1)}, s32[1,2,2048]{2,1,0:T(2,128)}, u32[]{:S(2)}) copy-start(s32[1,2,2048]{2,1,0:T(2,128)} %param.17) | copy-start | bytes 49156
  119.4 3.9 %copy-start.2 = (bf16[1,4096,256]{2,1,0:T(8,128)(2,1)S(1)}, bf16[1,4096,256]{2,1,0:T(8,128)(2,1)}, u32[]{:S(2)}) copy-start(bf16[1,4096,256]{2,1,0:T(8,128)(2,1)} %shard_map.141) | copy-start | bytes 6291460
  119.4 3.9 %copy-start.5 = (bf16[1,32,4096]{2,1,0:T(8,128)(2,1)S(1)}, bf16[1,32,4096]{2,1,0:T(8,128)(2,1)}, u32[]{:S(2)}) copy-start(bf16[1,32,4096]{2,1,0:T(8,128)(2,1)} %param.20) | copy-start | bytes 786436
  123.3 18.9 %copy-start.9 = (s32[1,2048]{1,0:T(1,128)S(1)}, s32[1,2048]{1,0:T(1,128)}, u32[]{:S(2)}) copy-start(s32[1,2048]{1,0:T(1,128)} %param.21) | copy-start | bytes 24580
  124.4 54.5 %copy-start.6 = (bf16[128,1024]{1,0:T(8,128)(2,1)S(1)}, bf16[128,1024]{1,0:T(8,128)(2,1)}, u32[]{:S(2)}) copy-start(bf16[128,1024]{1,0:T(8,128)(2,1)} %param.22) | copy-start | bytes 786436

commit v4 on v3

--- a/solution.py
+++ b/solution.py
@@ -8,7 +8,6 @@
 from jax.sharding import PartitionSpec as P
 
 MESH_ID = pl.DeviceIdType.MESH
-RELAY = False
 
 
 def ring_hops(n, plus_longer):
@@ -16,7 +15,7 @@
     return (longer, shorter) if plus_longer else (shorter, longer)
 
 
-def spread_kernel(reduced, negated, first, second, paired, first_stride, second_stride, *refs):
+def spread_kernel(relayed, reduced, negated, first, second, paired, first_stride, second_stride, *refs):
     x_ref = refs[0]
     base_ref = refs[1] if negated else None
     o_ref = refs[1 + negated]
@@ -26,7 +25,6 @@
     n_first = lax.axis_size(first) if first else 1
     ways = 2 if paired else 1
     n_second = lax.axis_size(second) // ways
-    relayed = RELAY and n_second <= 4
     me_first = lax.axis_index(first) if first else 0
     index = lax.axis_index(second)
     core = lax.rem(index, ways)
@@ -108,7 +106,8 @@
         src = x_ref
 
     order = sorted(range(1, n_first), key=lambda d: min(d, n_first - d))
-    for d in order:
+    hybrid = relayed and n_first == 8
+    for d in (1, 7, 2, 6) if hybrid else order:
         send(src, own, first_send.at[d - 1], first_recv.at[d - 1], {first: at_first(d)})
 
     far_first = sorted(range(1, n_second), key=lambda d: -min(d, n_second - d))
@@ -142,21 +141,38 @@
             send(here, here, mate_send.at[j, d], mate_recv.at[j, d], mate)
 
     start_second(0, src, own)
-    for j in range(1, n_first):
+    def take_first(j):
         d = steps[j]
         here = slot(at_first(-d), index)
         arrived(here, first_send.at[d - 1], first_recv.at[d - 1], {first: at_first(d)})
+        if hybrid:
+            for further in {2: (3, 4), 6: (5,)}.get(d, ()):
+                send(
+                    here,
+                    here,
+                    first_send.at[further - 1],
+                    first_recv.at[further - 1],
+                    {first: at_first(further - d)},
+                )
         start_second(j, here, here)
-    if relayed:
-        for k in range(1, n_second // 2 + 1):
-            for j in range(n_first):
-                for direction, limit in zip((1, -1), ring_hops(n_second, j % 2 == 0)):
-                    if k <= limit:
-                        take_second(j, direction, k, limit)
-    else:
+
+    depth = n_second // 2
+
+    def take_hop(j, k):
+        if relayed:
+            for direction, limit in zip((1, -1), ring_hops(n_second, j % 2 == 0)):
+                if k <= limit:
+                    take_second(j, direction, k, limit)
+        else:
+            for d in far_first[::-1]:
+                if min(d, n_second - d) == k:
+                    take_second(j, d, 1, 1)
+
+    for j in range(1, n_first):
+        take_first(j)
+    for k in range(1, depth + 1):
         for j in range(n_first):
-            for d in far_first[::-1]:
-                take_second(j, d, 1, 1)
+            take_hop(j, k)
     if paired:
         for j in range(n_first):
             for d in range(n_second):
@@ -168,7 +184,18 @@
         keep.wait()
 
 
-def spread(x, reduced, first, second, paired, first_stride, second_stride, collective_id, base=None):
+def spread(
+    x,
+    reduced,
+    first,
+    second,
+    paired,
+    first_stride,
+    second_stride,
+    collective_id,
+    base=None,
+    relayed=False,
+):
     lead, height, width = x.shape[-3:]
     n_first = lax.axis_size(first) if first else 1
     n_devices = n_first * lax.axis_size(second)
@@ -181,7 +208,15 @@
         scratch += [pltpu.VMEM((n,) + x.shape[1:], x.dtype), dma((n,)), dma((n,))]
     operands = (x,) if base is None else (x, base)
     body = functools.partial(
-        spread_kernel, reduced, base is not None, first, second, paired, first_stride, second_stride
+        spread_kernel,
+        relayed,
+        reduced,
+        base is not None,
+        first,
+        second,
+        paired,
+        first_stride,
+        second_stride,
     )
     return pl.pallas_call(
         body,
@@ -224,7 +259,9 @@
     ).astype(jnp.bfloat16)
     own_rows = child_rows // n_col
     part = part.reshape(children, n_col, own_rows, width).transpose(1, 0, 2, 3)
-    child_whole = spread(part, "col", "row", "col", True, child_rows, own_rows, 0)
+    child_whole = spread(
+        part, "col", "row", "col", True, child_rows, own_rows, 0, relayed=True
+    )
     child_local = lax.dynamic_slice_in_dim(child_whole, row * child_rows, child_rows, 1)
 
     update_mid = jnp.einsum(
@@ -235,7 +272,9 @@
     ).astype(jnp.bfloat16)
     piece = update_mid.shape[1]
     stacked = jnp.concatenate((update_mid, update_root), axis=0)
-    updates = spread(stacked, None, "row", "col", True, n_col * piece, piece, 1)
+    updates = spread(
+        stacked, None, "row", "col", True, n_col * piece, piece, 1, relayed=True
+    )
 
     mid_rows = mid_rhs.shape[1]
     mid_term = placed_sum(updates[:children], mid_rows_list, col * mid_rows, mid_rows)

time: 197 us -> 194 us (0.985)
  Pallas kernels: 167 us -> 164 us
    pallas_call x6, Pallas kernels: 167 us -> 164 us  [spread(): pl.pallas_call(body, out_shape=jax.ShapeDtypeStruct((lead, height * n_dev...]
where the time goes in v4:
time: 194 us; the launch traced here: 193 us
  Pallas kernels  164 us (85%)
  matrix products  14.5 us (7%)
  local copies, waits for them, and re-layouts  13.1 us (7%)
    pallas_call x6, Pallas kernels, spread(): pl.pallas_call(body, out_shape=jax.ShapeDtypeStruct((lead, height * n_dev...  164 us
    dot_general x2, matrix products, placed_sum(): return jnp.dot(picks, flat, preferred_element_type=jnp.float32)  4.2 us

profile of v4, /device:TPU:1, one launch (start us, length us, event | category | flops | bytes accessed | tf_op | source)
XLA Modules:
  0.0 193.2 jit_solution(2750770918218513018)
XLA Ops:
  0.6 1.1 copy-done
  1.7 1.4 convolution_convert_fusion
  3.1 0.8 copy.21
  3.8 37.9 %shard_map.139 = bf16[2,3072,256]{2,1,0:T(8,128)(2,1)} custom-call(bf16[8,2,48,256]{3,2,1,0:T(8,128)(2,1)} %bitcast.77), custom_call_target="tpu_custom_call" | custom-call | tf_op jit(solution)/shard_map/pallas_call | solution.py:221
  41.7 1.9 dynamic-slice_bitcast_fusion
  43.7 2.5 %fusion.9 = bf16[2,32,256]{2,1,0:T(8,128)(2,1)S(1)} fusion(bf16[2,3072,256]{2,1,0:T(8,128)(2,1)} %shard_map.139, bf16[1,2,32,3072]{3,2,1,0:T(8,128)(2,1)S(1)} %copy-done.3), kind=kOutput, calls=%fused_computation.16 | convolution fusion | flops 100679680 | bytes 3571712 | tf_op jit(solution)/shard_map/cuj,cjr->cur/dot_general | solution.py:270
  46.2 0.0 copy-done.1
  46.2 0.6 fusion.8
  46.9 0.6 pad_maximum_fusion.refs_0_
  47.5 31.7 %shard_map.140 = bf16[4,2048,256]{2,1,0:T(8,128)(2,1)} custom-call(bf16[4,32,256]{2,1,0:T(8,128)(2,1)} %pad_maximum_fusion.refs_0_), custom_call_target="tpu_custom_call" | custom-call | tf_op jit(solution)/shard_map/pallas_call | solution.py:221
  79.2 3.9 %fusion.29 = (bf16[2,2048,256]{2,1,0:T(8,128)(2,1)}, bf16[2,2048,256]{2,1,0:T(8,128)(2,1)S(1)}) fusion(bf16[4,2048,256]{2,1,0:T(8,128)(2,1)} %shard_map.140), kind=kLoop, calls=%fused_computation.41 | loop fusion | bytes 8388608 | tf_op jit(solution)/shard_map/slice | solution.py:298
  83.1 2.8 %fusion.7 = bf16[512,256]{0,1:T(8,128)(2,1)S(1)} fusion(bf16[4096,256]{1,0:T(8,128)(2,1)S(1)} %bitcast.76, s32[4096]{0:T(1024)S(1)} %bitcast.84, bf16[1,512,512]{2,1,0:T(8,128)(2,1)S(1)} %copy-done.10, bf16[1,512,256]{2,1,0:T(8,128)(2,1)} %param.19), kind=kOutput, calls=%fused_computation.11 | convolution fusion | flops 1210580992 | bytes 3162112 | tf_op jit(solution)/shard_map/dot_general | solution.py:282
  85.9 0.8 copy.17
  86.8 28.6 %shard_map.141 = bf16[1,4096,256]{2,1,0:T(8,128)(2,1)} custom-call(bf16[8,1,64,256]{3,2,1,0:T(8,128)(2,1)} %bitcast.79), custom_call_target="tpu_custom_call" | custom-call | tf_op jit(solution)/shard_map/pallas_call | solution.py:221
  115.4 1.8 constant_dynamic-slice_fusion
  117.2 2.0 %fusion.4 = f32[128,256]{1,0:T(8,128)S(1)} fusion(bf16[4096,256]{1,0:T(8,128)(2,1)} %bitcast.75, s32[4096]{0:T(1024)S(1)} %bitcast.85), kind=kOutput, calls=%fused_computation.6 | convolution fusion | flops 268959744 | bytes 2244608 | tf_op jit(solution)/shard_map/dot_general | solution.py:235
  119.3 1.1 fusion.13.refs_0_
  120.4 17.4 %shard_map.142 = bf16[1,2048,256]{2,1,0:T(8,128)(2,1)} custom-call(bf16[1,32,256]{2,1,0:T(8,128)(2,1)} %fusion.13.refs_0_), custom_call_target="tpu_custom_call" | custom-call | tf_op jit(solution)/shard_map/pallas_call | solution.py:221
  137.8 2.2 %convolution_add_fusion = f32[128,256]{1,0:T(8,128)} fusion(f32[128,256]{1,0:T(8,128)S(1)} %fusion.4, bf16[1,2048,256]{2,1,0:T(8,128)(2,1)} %shard_map.142, s32[2048]{0:T(1024)S(1)} %bitcast.83), kind=kOutput, calls=%fused_computation.12 | convolution fusion | flops 134512640 | bytes 1318912 | tf_op jit(solution)/shard_map/dot_general | solution.py:235
  140.0 1.3 dynamic-slice_bitcast_fusion.1.refs_1_
  141.3 33.1 %shard_map.143 = bf16[1,1024,256]{2,1,0:T(8,128)(2,1)} custom-call(f32[8,1,16,256]{3,2,1,0:T(8,128)} %bitcast.81, bf16[1,16,256]{2,1,0:T(8,128)(2,1)} %dynamic-slice_bitcast_fusion.1.refs_1_), custom_call_target="tpu_custom_call" | custom-call | tf_op jit(solution)/shard_map/pallas_call | solution.py:221
  174.4 1.9 fusion.20
  176.4 15.4 %shard_map.144 = bf16[1,128,256]{2,1,0:T(8,128)(2,1)} custom-call(f32[8,1,16,256]{3,2,1,0:T(8,128)} %bitcast.80), custom_call_target="tpu_custom_call" | custom-call | tf_op jit(solution)/shard_map/pallas_call | solution.py:221
  191.8 1.5 copy.23
  (25 shorter events, 0.1 us)
Async XLA Ops:
  0.6 1.1 copy-start
  3.8 39.8 %copy-start.3 = (bf16[1,2,32,3072]{3,2,1,0:T(8,128)(2,1)S(1)}, bf16[1,2,32,3072]{3,2,1,0:T(8,128)(2,1)}, u32[]{:S(2)}) copy-start(bf16[1,2,32,3072]{3,2,1,0:T(8,128)(2,1)} %param.15) | copy-start | bytes 1179652
  41.7 4.5 %copy-start.1 = (bf16[2,3072,256]{2,1,0:T(8,128)(2,1)S(1)}, bf16[2,3072,256]{2,1,0:T(8,128)(2,1)}, u32[]{:S(2)}) copy-start(bf16[2,3072,256]{2,1,0:T(8,128)(2,1)} %shard_map.139) | copy-start | bytes 9437188
  41.7 4.5 %copy-start.4 = (bf16[1,2,32,3072]{3,2,1,0:T(8,128)(2,1)S(1)}, bf16[1,2,32,3072]{3,2,1,0:T(8,128)(2,1)}, u32[]{:S(2)}) copy-start(bf16[1,2,32,3072]{3,2,1,0:T(8,128)(2,1)} %param.14) | copy-start | bytes 1179652
  79.2 3.9 %copy-start.7 = (s32[1,2,2048]{2,1,0:T(2,128)S(1)}, s32[1,2,2048]{2,1,0:T(2,128)}, u32[]{:S(2)}) copy-start(s32[1,2,2048]{2,1,0:T(2,128)} %param.16) | copy-start | bytes 49156
  79.2 3.9 %copy-start.10 = (bf16[1,512,512]{2,1,0:T(8,128)(2,1)S(1)}, bf16[1,512,512]{2,1,0:T(8,128)(2,1)}, u32[]{:S(2)}) copy-start(bf16[1,512,512]{2,1,0:T(8,128)(2,1)} %param.18) | copy-start | bytes 1572868
  85.9 31.3 %copy-start.8 = (s32[1,2,2048]{2,1,0:T(2,128)S(1)}, s32[1,2,2048]{2,1,0:T(2,128)}, u32[]{:S(2)}) copy-start(s32[1,2,2048]{2,1,0:T(2,128)} %param.17) | copy-start | bytes 49156
  115.4 3.9 %copy-start.2 = (bf16[1,4096,256]{2,1,0:T(8,128)(2,1)S(1)}, bf16[1,4096,256]{2,1,0:T(8,128)(2,1)}, u32[]{:S(2)}) copy-start(bf16[1,4096,256]{2,1,0:T(8,128)(2,1)} %shard_map.141) | copy-start | bytes 6291460
  115.4 3.9 %copy-start.5 = (bf16[1,32,4096]{2,1,0:T(8,128)(2,1)S(1)}, bf16[1,32,4096]{2,1,0:T(8,128)(2,1)}, u32[]{:S(2)}) copy-start(bf16[1,32,4096]{2,1,0:T(8,128)(2,1)} %param.20) | copy-start | bytes 786436
  119.3 18.5 %copy-start.9 = (s32[1,2048]{1,0:T(1,128)S(1)}, s32[1,2048]{1,0:T(1,128)}, u32[]{:S(2)}) copy-start(s32[1,2048]{1,0:T(1,128)} %param.21) | copy-start | bytes 24580
  120.4 54.0 %copy-start.6 = (bf16[128,1024]{1,0:T(8,128)(2,1)S(1)}, bf16[128,1024]{1,0:T(8,128)(2,1)}, u32[]{:S(2)}) copy-start(bf16[128,1024]{1,0:T(8,128)(2,1)} %param.22) | copy-start | bytes 786436
